TPU v7x, 512 devices: a whole 4x4x16 slice. The times are simulated.
512 devices in a mesh: row: 32 (over x, y, core), col: 16 (over z).
Axes of the slice: x: 4, y: 4, z: 16, core: 2. Of those that a mesh axis runs over, the one named last changes fastest.
Arguments:
- features: bfloat16 [3, 32, 128, 512], P(None, 'row', 'col'), may hold values from -6 to 6
Outputs:
- panels: float32 [3, 32, 128, 256], P(None, 'row')
- trailing: float32 [3, 32, 128, 6, 16, 128], P(None, 'row', None, None, 'col')
All inputs are finite; a program needn't handle non-finite values.
Results may differ from a plain program's by a relative error of at most 0.0003.
Values may be sent and summed in bfloat16 or wider, within the bound.
A program may use at most 64 MiB of HBM per device.

v0:
```python
import functools, math
import jax, jax.numpy as jnp
from jax import lax
from jax.experimental import pallas as pl
from jax.experimental.pallas import tpu as pltpu
from jax.sharding import PartitionSpec as P
MESH = pl.DeviceIdType.MESH
NZ = 16

def comm_kernel(H, x_ref, R, C, Q, lsem, zrecv, zsend, crecv, csend, qrecv, qsend, lc_sem):
    r = lax.axis_index("row")
    z = lax.axis_index("col")
    core = r % 2
    y = (r // 2) % 4
    x = r // 8

    def rid(xx, yy, cc):
        return (((xx + 4) % 4) * 4 + ((yy + 4) % 4)) * 2 + cc

    own = pltpu.make_async_copy(x_ref.at[:, 0], R.at[z], lsem)
    own.start()
    bar = pltpu.get_barrier_semaphore()
    peers = []
    zs = [j for j in range(1, H + 1)] + [16 - j for j in range(1, H + 1)]
    for j in sorted(set(zs)):
        peers.append((r, (z + j) % 16))
    for j in (1, 2, 3):
        peers.append((rid(x, y + j, core), z))
        peers.append((rid(x + j, y, core), z))
    peers.append((rid(x, y, 1 - core), z))
    for p in peers:
        pl.semaphore_signal(bar, inc=1, device_id=p, device_id_type=MESH)
    pl.semaphore_wait(bar, len(peers))
    own.wait()

    def zcopy(o, d, j):
        return pltpu.make_async_remote_copy(
            src_ref=R.at[o], dst_ref=R.at[o], send_sem=zsend.at[(0 if d > 0 else H) + j - 1],
            recv_sem=zrecv.at[o], device_id=(r, (z + d * j + 16) % 16), device_id_type=MESH)

    xs0, ys, cs = z // 8, (z // 2) % 4, z % 2
    streams = []
    for t in range(2):
        streams.append((qrecv, qsend, t, Q, 0, 0, t))
    for b in range(2):
        streams.append((crecv, csend, b, C, xs0 + 2 * b, ys, cs))

    def targets():
        ts = [(rid(x, y + j, core), z) for j in (1, 2, 3)]
        ts += [(rid(x + j, y, core), z) for j in (1, 2, 3)]
        ts += [(rid(x, y, 1 - core), z)]
        return ts

    def src_of(S, o):
        rs, ss, i, buf, rx, ry, rc = S
        return R.at[o, 0] if buf is Q else R.at[o]

    def pcopy(S, o, k, src):
        rs, ss, i, buf, rx, ry, rc = S
        return pltpu.make_async_remote_copy(
            src_ref=src, dst_ref=buf.at[i, o], send_sem=ss.at[i, k], recv_sem=rs.at[i, o],
            device_id=targets()[k], device_id_type=MESH)

    def roles(S):
        rs, ss, i, buf, rx, ry, rc = S
        oncore = core == rc
        is_src = oncore & (x == rx) & (y == ry)
        is_y = oncore & (x == rx) & (y != ry)
        is_x = oncore & (x != rx)
        is_s = core != rc
        return is_src, is_y, is_x, is_s

    def local_copy(S, o):
        rs, ss, i, buf, rx, ry, rc = S
        return pltpu.make_async_copy(src_of(S, o), buf.at[i, o], rs.at[i, o])

    def at_source(o):
        for S in streams:
            @pl.when(roles(S)[0])
            def _():
                for k in range(7):
                    pcopy(S, o, k, src_of(S, o)).start()
                local_copy(S, o).start()

    def wait_block(S, o):
        rs, ss, i, buf, rx, ry, rc = S
        pltpu.make_async_copy(buf.at[i, o], buf.at[i, o], rs.at[i, o]).wait()

    def relay(which, o):
        for S in streams:
            role = roles(S)[which]
            buf, i = S[3], S[2]
            @pl.when(role)
            def _():
                wait_block(S, o)
                ks = {1: (3, 4, 5, 6), 2: (6,), 3: ()}[which]
                for k in ks:
                    pcopy(S, o, k, buf.at[i, o]).start()

    for j in range(1, H + 1):
        zcopy(z, 1, j).start()
        if j <= 7:
            zcopy(z, -1, j).start()
    at_source(z)

    def seq(i):
        d = (i + 1) // 2
        return lax.rem(jnp.where(i % 2 == 1, z - d, z + d) + 16, 16)

    def step(i, _):
        @pl.when((i >= 1) & (i < 16))
        def _():
            o = seq(i)
            d = (i + 1) // 2
            pltpu.make_async_copy(R.at[o], R.at[o], zrecv.at[o]).wait()
            fwd = (d % H == 0)
            @pl.when(fwd & (i % 2 == 1))
            def _():
                for j in range(1, H + 1):
                    @pl.when(d + j <= 8)
                    def _():
                        zcopy(o, 1, j).start()
            @pl.when(fwd & (i % 2 == 0))
            def _():
                for j in range(1, min(H, 7) + 1):
                    @pl.when(d + j <= 7)
                    def _():
                        zcopy(o, -1, j).start()
            at_source(o)
        for which, lag in ((1, 2), (2, 4), (3, 5)):
            @pl.when((i >= lag) & (i < 16 + lag))
            def _():
                relay(which, seq(i - lag))
        return 0

    lax.fori_loop(0, 21, step, 0)

    for S in streams:
        @pl.when(roles(S)[0])
        def _():
            def w(o, _):
                wait_block(S, o)
                return 0
            lax.fori_loop(0, 16, w, 0)
    for d, lim in ((1, 8), (-1, 7)):
        for j in range(1, H + 1):
            n = (1 if j <= lim else 0) + sum(1 for dd in range(H, lim, H) if dd + j <= lim)
            if n:
                v = R.at[pl.ds(0, n)]
                pltpu.make_async_copy(v, v, zsend.at[(0 if d > 0 else H) + j - 1]).wait()
    for S in streams:
        rs, ss, i, buf, rx, ry, rc = S
        is_src, is_y, is_x, is_s = roles(S)
        for k in range(7):
            cond = is_src if k < 3 else ((is_src | is_y) if k < 6 else (core == rc))
            @pl.when(cond)
            def _():
                pltpu.make_async_copy(buf.at[i], buf.at[i], ss.at[i, k]).wait()


def gather(features, H=1):
    vm = pl.BlockSpec(memory_space=pltpu.VMEM)
    return pl.pallas_call(
        functools.partial(comm_kernel, H),
        out_shape=(jax.ShapeDtypeStruct((16, 3, 8, 512), jnp.bfloat16),
                   jax.ShapeDtypeStruct((2, 16, 3, 8, 512), jnp.bfloat16),
                   jax.ShapeDtypeStruct((2, 16, 8, 512), jnp.bfloat16)),
        in_specs=[pl.BlockSpec(memory_space=pl.ANY)],
        out_specs=(vm, vm, vm),
        scratch_shapes=[pltpu.SemaphoreType.DMA, pltpu.SemaphoreType.DMA((16,)), pltpu.SemaphoreType.DMA((2 * H,)),
                        pltpu.SemaphoreType.DMA((2, 16)), pltpu.SemaphoreType.DMA((2, 7)),
                        pltpu.SemaphoreType.DMA((2, 16)), pltpu.SemaphoreType.DMA((2, 7)),
                        pltpu.SemaphoreType.DMA],
        compiler_params=pltpu.CompilerParams(collective_id=0, has_side_effects=True),
        name="gather_features",
    )(features)


F = 512
F32 = jnp.float32
BF = jnp.bfloat16
IPI = 1.0 / math.pi
POLY = (1.5707963050, -0.2145988016, 0.0889789874, -0.0501743046,
        0.0308918810, -0.0170881256, 0.0066700901, -0.0012624911)
NT = (((1,), (1,)), ((), ()))
NN = (((1,), (0,)), ((), ()))
TN = (((0,), (0,)), ((), ()))


def dot(a, b, dims):
    return lax.dot_general(a, b, dims, preferred_element_type=F32)


def split(a):
    hi = a.astype(BF)
    return hi, (a - hi.astype(F32)).astype(BF)


def dot3(a, b, dims):
    return dot(a[0], b[0], dims) + (dot(a[0], b[1], dims) + dot(a[1], b[0], dims))


def half_angle(ax):
    y = jnp.maximum(1.0 - ax, 1e-30)
    s = y * lax.rsqrt(y)
    z = 1.0 + ax
    root = (s * IPI) * (z * lax.rsqrt(z))
    p = POLY[7] * IPI
    for c in POLY[6::-1]:
        p = p * ax + c * IPI
    return root, s * p


def ntk(gram, ur, uc, scale):
    t = gram * (ur * uc)
    root, w = half_angle(jnp.abs(t))
    h = jnp.where(t < 0.0, w, 1.0 - w)
    th = t * h
    jf = root + th
    theta = th + jf
    root2, w2 = half_angle(jnp.minimum(jf, 1.0))
    h2 = 1.0 - w2
    return (root2 + h2 * (theta + jf)) * scale


def squares(x):
    x = x.astype(F32)
    return split(x * x)


def col_form(sq):
    ones = jnp.ones((128, F), BF)
    return (dot(sq[0], ones, NT) + dot(sq[1], ones, NT)) * (1.0 / F) + 1e-6


def row_form(sq):
    ones = jnp.ones((8, F), BF)
    return (dot(ones, sq[0], NT) + dot(ones, sq[1], NT))[0:1] * (1.0 / F) + 1e-6


def full_kernel(B, R, C, Q, out_l, out_t, xr, xc, xp, qr, qc, qcr, qpr, qpc, M, kr, kc, oslot, osem):
    r = lax.axis_index("row")
    z = lax.axis_index("col")
    N = 256
    for t in range(2):
        v = Q[t].reshape(128, F)
        xp[t * 128:(t + 1) * 128] = v
        sq = squares(v)
        qpc[t * 128:(t + 1) * 128] = col_form(sq)
        qpr[:, t * 128:(t + 1) * 128] = row_form(sq)
    for a in range(3):
        v = R[:, a].reshape(128, F)
        xr[a * 128:(a + 1) * 128] = v
        qr[a * 128:(a + 1) * 128] = col_form(squares(v))
        for b in range(2):
            t = 2 * a + b
            v = C[b, :, a].reshape(128, F)
            xc[t * 128:(t + 1) * 128] = v
            sq = squares(v)
            qc[t * 128:(t + 1) * 128] = col_form(sq)
            qcr[:, t * 128:(t + 1) * 128] = row_form(sq)
    ii = lax.broadcasted_iota(jnp.int32, (128, 128), 0)
    jj = lax.broadcasted_iota(jnp.int32, (128, 128), 1)

    def tile(xa, qa, xb, qb, same):
        gram = dot(xa, xb, NT) * (1.0 / F)
        k = ntk(gram, lax.rsqrt(qa), lax.rsqrt(qb), jnp.sqrt(qa) * jnp.sqrt(qb))
        if same is False:
            return k
        eq = ii == jj if same is True else (ii == jj) & same
        return jnp.where(eq, gram + 2.0 * qa + 1.0, k)

    def at(ref, i):
        return ref[pl.ds(pl.multiple_of(i * 128, 128), 128)]

    for i in range(2):
        for t in range(2):
            M[i * 128:(i + 1) * 128, t * 128:(t + 1) * 128] = tile(
                at(xp, i), at(qpc, i), at(xp, t), qpr[:, t * 128:(t + 1) * 128], i == t)
    ri = lax.broadcasted_iota(jnp.int32, (N, N), 0)
    ci = lax.broadcasted_iota(jnp.int32, (N, N), 1)
    M[:, N:2 * N] = jnp.where(ri == ci, 1.0, 0.0)

    bi = lax.broadcasted_iota(jnp.int32, (B, B), 0)
    bj = lax.broadcasted_iota(jnp.int32, (B, B), 1)
    b2i = lax.broadcasted_iota(jnp.int32, (B, 2 * B), 0)
    for n in range(N // B):
        lo = n * B
        S = jnp.concatenate([M[lo:lo + B, lo:lo + B], jnp.where(bi == bj, 1.0, 0.0)], axis=1)
        dinv = jnp.zeros((B, 1), F32)
        for j in range(B):
            d = lax.rsqrt(S[j:j + 1, j:j + 1])
            row = S[j:j + 1, :] * d
            colv = S[:, j:j + 1] * d
            below = b2i > j
            S = jnp.where(below, S - colv * row, jnp.where(b2i == j, row, S))
        w = split(S[:, B:])
        Y = dot3(w, split(M[lo:lo + B, :]), NN)
        M[lo:lo + B, :] = Y
        if lo + B < N:
            ys = split(Y)
            U = split(Y[:, lo + B:N])
            M[lo + B:, lo + B:] = M[lo + B:, lo + B:] - dot3(U, tuple(v[:, lo + B:] for v in ys), TN)
    w = split(M[:, N:])

    for i in range(3):
        for t in range(2):
            kr[i * 128:(i + 1) * 128, t * 128:(t + 1) * 128] = tile(
                at(xr, i), at(qr, i), at(xp, t), qpr[:, t * 128:(t + 1) * 128],
                (r == t) if i == 0 else False)
    for i in range(6):
        for t in range(2):
            kc[i * 128:(i + 1) * 128, t * 128:(t + 1) * 128] = tile(
                at(xc, i), at(qc, i), at(xp, t), qpr[:, t * 128:(t + 1) * 128],
                (z == t) if i == 0 else False)
    lr = dot3(split(kr[...]), w, NT)
    out_l[...] = lr
    lc = dot3(split(kc[...]), w, NT)
    lr = split(lr)
    lc = split(lc)
    for a in range(3):
        rows = slice(a * 128, (a + 1) * 128)
        for t in range(6):
            cols = slice(t * 128, (t + 1) * 128)
            b = t % 2
            k = tile(at(xr, a), at(qr, a), at(xc, t), qcr[:, cols],
                     (r == z + 16 * b) if t // 2 == a else False)
            k = k - dot3(tuple(v[rows] for v in lr), tuple(v[cols] for v in lc), NT)
            oslot[t, rows] = k
    copies = []
    for a in range(3):
        for t in range(6):
            c = pltpu.make_async_copy(oslot.at[t, pl.ds(a * 128, 128)], out_t.at[a, 0, :, t, 0, :], osem.at[a, t])
            c.start()
            copies.append(c)
    for c in copies:
        c.wait()


def compute(R, C, Q, B=32, interpret=False):
    vm = pl.BlockSpec(memory_space=pltpu.VMEM)
    out_l, out_t = pl.pallas_call(
        functools.partial(full_kernel, B),
        out_shape=(jax.ShapeDtypeStruct((384, 256), F32),
                   jax.ShapeDtypeStruct((3, 1, 128, 6, 1, 128), F32)),
        in_specs=[vm] * 3,
        out_specs=(vm, pl.BlockSpec(memory_space=pl.ANY)),
        scratch_shapes=[pltpu.VMEM((384, F), BF), pltpu.VMEM((768, F), BF), pltpu.VMEM((256, F), BF),
                        pltpu.VMEM((384, 128), F32), pltpu.VMEM((768, 128), F32), pltpu.VMEM((1, 768), F32),
                        pltpu.VMEM((1, 256), F32), pltpu.VMEM((256, 128), F32), pltpu.VMEM((256, 512), F32),
                        pltpu.VMEM((384, 256), F32), pltpu.VMEM((768, 256), F32), pltpu.VMEM((6, 384, 128), F32),
                        pltpu.SemaphoreType.DMA((3, 6))],
        name="panel_kernel", interpret=interpret,
    )(R, C, Q)
    return out_l.reshape(3, 1, 128, 256), out_t


def local(features):
    R, C, Q = gather(features, 2)
    return compute(R, C, Q, 32)


def solution(mesh):
    return jax.shard_map(
        local,
        mesh=mesh,
        in_specs=(P(None, "row", "col", None),),
        out_specs=(P(None, "row", None, None), P(None, "row", None, None, "col", None)),
        check_vma=False,
    )
```

profile of v0, /device:TPU:25, one launch (start us, length us, event | category | flops | bytes accessed | tf_op | source)
XLA Modules:
  0.0 81.3 jit_solution(4306505758549842361)
XLA Ops:
  0.6 43.9 %gather_features.1 = (bf16[16,3,8,512]{3,2,1,0:T(8,128)(2,1)}, bf16[2,16,3,8,512]{4,3,2,1,0:T(8,128)(2,1)}, bf16[2,16,8,512]{3,2,1,0:T(8,128)(2,1)}) custom-call(bf16[3,1,8,512]{3,2,1,0:T(8,128)(2,1)} %x_ref.1), custom_call_target="tpu_custom_call" | custom-call | tf_op jit(solution)/shard_map/gather_features/pallas_call | solution.py:163
  44.5 36.8 %panel_kernel.1 = (f32[384,256]{1,0:T(8,128)}, f32[3,1,128,6,1,128]{5,4,3,2,1,0:T(1,128)}) custom-call(bf16[16,3,8,512]{3,2,1,0:T(8,128)(2,1)} %get-tuple-element.7.R, bf16[2,16,3,8,512]{4,3,2,1,0:T(8,128)(2,1)} %get-tuple-element.8.C, bf16[2,16,8,512]{3,2,1,0:T(8,128)(2,1)} %get-tuple-element.9.Q), custom_call_target="tpu_custom_call" | custom-call | tf_op jit(solution)/shard_map/panel_kernel/pallas_call | solution.py:342
where the time goes:
time: 81.8 us; the launch traced here: 81.3 us
  Pallas kernels  80.6 us (99%)
    pallas_call x1, Pallas kernels, gather(): pl.pallas_call(functools.partial(comm_kernel, H), out_shape=(jax.ShapeDty...  43.9 us
    pallas_call x1, Pallas kernels, compute(): pl.pallas_call(functools.partial(full_kernel, B), out_shape=(jax.ShapeDty...  36.8 us

commit v1 on v0

--- a/solution.py
+++ b/solution.py
@@ -238,7 +238,7 @@
     return (dot(ones, sq[0], NT) + dot(ones, sq[1], NT))[0:1] * (1.0 / F) + 1e-6
 
 
-def full_kernel(B, R, C, Q, out_l, out_t, xr, xc, xp, qr, qc, qcr, qpr, qpc, M, kr, kc, oslot, osem):
+def full_kernel(B, skip, R, C, Q, out_l, out_t, xr, xc, xp, qr, qc, qcr, qpr, qpc, M, kr, kc, oslot, osem):
     r = lax.axis_index("row")
     z = lax.axis_index("col")
     N = 256
@@ -281,34 +281,52 @@
     ci = lax.broadcasted_iota(jnp.int32, (N, N), 1)
     M[:, N:2 * N] = jnp.where(ri == ci, 1.0, 0.0)
 
-    bi = lax.broadcasted_iota(jnp.int32, (B, B), 0)
-    bj = lax.broadcasted_iota(jnp.int32, (B, B), 1)
-    b2i = lax.broadcasted_iota(jnp.int32, (B, 2 * B), 0)
-    for n in range(N // B):
+    sub = lax.broadcasted_iota(jnp.int32, (8, 128), 0)
+    G = B // 8
+
+    def wide(v):
+        return jnp.broadcast_to(v, (8, 128))
+
+    for n in range(0 if 'C' in skip else N // B):
         lo = n * B
-        S = jnp.concatenate([M[lo:lo + B, lo:lo + B], jnp.where(bi == bj, 1.0, 0.0)], axis=1)
-        dinv = jnp.zeros((B, 1), F32)
-        for j in range(B):
-            d = lax.rsqrt(S[j:j + 1, j:j + 1])
-            row = S[j:j + 1, :] * d
-            colv = S[:, j:j + 1] * d
-            below = b2i > j
-            S = jnp.where(below, S - colv * row, jnp.where(b2i == j, row, S))
-        w = split(S[:, B:])
-        Y = dot3(w, split(M[lo:lo + B, :]), NN)
-        M[lo:lo + B, :] = Y
-        if lo + B < N:
-            ys = split(Y)
-            U = split(Y[:, lo + B:N])
-            M[lo + B:, lo + B:] = M[lo + B:, lo + B:] - dot3(U, tuple(v[:, lo + B:] for v in ys), TN)
+        hi = lo + B
+        D = M[lo:hi, lo // 128 * 128:lo // 128 * 128 + 128]
+        o = lo % 128
+        col = [[wide(D[8 * g:8 * g + 8, o + k:o + k + 1]) if g >= k // 8 else None for g in range(G)]
+               for k in range(B)]
+        lanes = list(range(hi // 128, 2)) + list(range(2, 3 + (hi - 1) // 128))
+        S = [[M[lo + 8 * g:lo + 8 * g + 8, 128 * v:128 * v + 128] for v in lanes] for g in range(G)]
+        for k in range(0 if 'c' in skip else B):
+            gk = k // 8
+            rs = wide(lax.rsqrt(col[k][gk])[k % 8:k % 8 + 1])
+            c = [col[k][g] * rs if g >= gk else None for g in range(G)]
+            for m in range(k + 1, B):
+                f = wide(c[m // 8][m % 8:m % 8 + 1])
+                for g in range(m // 8, G):
+                    col[m][g] = col[m][g] - c[g] * f
+            below = jnp.where(sub > k % 8, c[gk], 0.0)
+            for v in range(len(lanes)):
+                row = wide(S[gk][v][k % 8:k % 8 + 1]) * rs
+                S[gk][v] = jnp.where(sub == k % 8, row, S[gk][v] - below * row)
+                for g in range(gk + 1, G):
+                    S[g][v] = S[g][v] - c[g] * row
+        Y = [jnp.concatenate([S[g][v] for g in range(G)], axis=0) for v in range(len(lanes))]
+        for v in range(len(lanes)):
+            M[lo:hi, 128 * lanes[v]:128 * lanes[v] + 128] = Y[v]
+        if hi < N:
+            ys = [split(y) for y in Y]
+            U = split(M[lo:hi, hi:N])
+            for v in range(len(lanes)):
+                cs = slice(128 * lanes[v], 128 * lanes[v] + 128)
+                M[hi:, cs] = M[hi:, cs] - dot3(U, ys[v], TN)
     w = split(M[:, N:])
 
-    for i in range(3):
+    for i in range(0 if 'k' in skip else 3):
         for t in range(2):
             kr[i * 128:(i + 1) * 128, t * 128:(t + 1) * 128] = tile(
                 at(xr, i), at(qr, i), at(xp, t), qpr[:, t * 128:(t + 1) * 128],
                 (r == t) if i == 0 else False)
-    for i in range(6):
+    for i in range(0 if 'k' in skip else 6):
         for t in range(2):
             kc[i * 128:(i + 1) * 128, t * 128:(t + 1) * 128] = tile(
                 at(xc, i), at(qc, i), at(xp, t), qpr[:, t * 128:(t + 1) * 128],
@@ -318,7 +336,8 @@
     lc = dot3(split(kc[...]), w, NT)
     lr = split(lr)
     lc = split(lc)
-    for a in range(3):
+    copies = []
+    for a in range(0 if 't' in skip else 3):
         rows = slice(a * 128, (a + 1) * 128)
         for t in range(6):
             cols = slice(t * 128, (t + 1) * 128)
@@ -326,33 +345,30 @@
             k = tile(at(xr, a), at(qr, a), at(xc, t), qcr[:, cols],
                      (r == z + 16 * b) if t // 2 == a else False)
             k = k - dot3(tuple(v[rows] for v in lr), tuple(v[cols] for v in lc), NT)
-            oslot[t, rows] = k
-    copies = []
-    for a in range(3):
-        for t in range(6):
-            c = pltpu.make_async_copy(oslot.at[t, pl.ds(a * 128, 128)], out_t.at[a, 0, :, t, 0, :], osem.at[a, t])
-            c.start()
-            copies.append(c)
+            oslot[pl.ds(a * 768 + t, 128, stride=6), :] = k
+        c = pltpu.make_async_copy(oslot.at[pl.ds(a * 768, 768)], out_t.at[pl.ds(a * 768, 768)], osem.at[a])
+        c.start()
+        copies.append(c)
     for c in copies:
         c.wait()
 
 
-def compute(R, C, Q, B=32, interpret=False):
+def compute(R, C, Q, B=32, interpret=False, skip=''):
     vm = pl.BlockSpec(memory_space=pltpu.VMEM)
     out_l, out_t = pl.pallas_call(
-        functools.partial(full_kernel, B),
+        functools.partial(full_kernel, B, skip),
         out_shape=(jax.ShapeDtypeStruct((384, 256), F32),
-                   jax.ShapeDtypeStruct((3, 1, 128, 6, 1, 128), F32)),
+                   jax.ShapeDtypeStruct((2304, 128), F32)),
         in_specs=[vm] * 3,
         out_specs=(vm, pl.BlockSpec(memory_space=pl.ANY)),
         scratch_shapes=[pltpu.VMEM((384, F), BF), pltpu.VMEM((768, F), BF), pltpu.VMEM((256, F), BF),
                         pltpu.VMEM((384, 128), F32), pltpu.VMEM((768, 128), F32), pltpu.VMEM((1, 768), F32),
                         pltpu.VMEM((1, 256), F32), pltpu.VMEM((256, 128), F32), pltpu.VMEM((256, 512), F32),
-                        pltpu.VMEM((384, 256), F32), pltpu.VMEM((768, 256), F32), pltpu.VMEM((6, 384, 128), F32),
-                        pltpu.SemaphoreType.DMA((3, 6))],
+                        pltpu.VMEM((384, 256), F32), pltpu.VMEM((768, 256), F32), pltpu.VMEM((2304, 128), F32),
+                        pltpu.SemaphoreType.DMA((3,))],
         name="panel_kernel", interpret=interpret,
     )(R, C, Q)
-    return out_l.reshape(3, 1, 128, 256), out_t
+    return out_l.reshape(3, 1, 128, 256), out_t.reshape(3, 1, 128, 6, 1, 128)
 
 
 def local(features):

time: 81.8 us -> 62.5 us (0.76)
  Pallas kernels: 80.6 us -> 61.4 us
    pallas_call x1, Pallas kernels: 36.8 us -> 17.5 us  [compute(): pl.pallas_call(functools.partial(full_kernel, B, skip), out_shape=(jax.Sh...]
where the time goes in v1:
time: 62.5 us; the launch traced here: 62 us
  Pallas kernels  61.4 us (98%)
  between operations  0.64 us (1%)
    pallas_call x1, Pallas kernels, gather(): pl.pallas_call(functools.partial(comm_kernel, H), out_shape=(jax.ShapeDty...  43.9 us
    pallas_call x1, Pallas kernels, compute(): pl.pallas_call(functools.partial(full_kernel, B, skip), out_shape=(jax.Sh...  17.5 us

profile of v1, /device:TPU:25, one launch (start us, length us, event | category | flops | bytes accessed | tf_op | source)
XLA Modules:
  0.0 62.0 jit_solution(17490092284281624241)
XLA Ops:
  0.6 43.9 %gather_features.1 = (bf16[16,3,8,512]{3,2,1,0:T(8,128)(2,1)}, bf16[2,16,3,8,512]{4,3,2,1,0:T(8,128)(2,1)}, bf16[2,16,8,512]{3,2,1,0:T(8,128)(2,1)}) custom-call(bf16[3,1,8,512]{3,2,1,0:T(8,128)(2,1)} %x_ref.1), custom_call_target="tpu_custom_call" | custom-call | tf_op jit(solution)/shard_map/gather_features/pallas_call | solution.py:163
  44.5 17.5 %panel_kernel.1 = (f32[384,256]{1,0:T(8,128)}, f32[2304,128]{1,0:T(8,128)}) custom-call(bf16[16,3,8,512]{3,2,1,0:T(8,128)(2,1)} %get-tuple-element.7.R, bf16[2,16,3,8,512]{4,3,2,1,0:T(8,128)(2,1)} %get-tuple-element.8.C, bf16[2,16,8,512]{3,2,1,0:T(8,128)(2,1)} %get-tuple-element.9.Q), custom_call_target="tpu_custom_call" | custom-call | tf_op jit(solution)/shard_map/panel_kernel/pallas_call | solution.py:358
